TPU v7x, 128 devices: a whole 4x4x4 slice. The times are simulated.
128 devices in a mesh: vocab: 16 (over z, x), width: 8 (over y, core).
Axes of the slice: x: 4, y: 4, z: 4, core: 2. Of those that a mesh axis runs over, the one named last changes fastest.
Arguments:
- hidden: bfloat16 [16384, 1024], P('vocab', 'width'), may hold values from -60 to 60
- norm_gain: float32 [1024], P('width'), may hold values from 0.5 to 1.5
- head_weight: bfloat16 [1024, 32128], P('width', 'vocab'), may hold values from -1 to 1
- token_ids: int32 [16384], P('width'), may hold values from 0 to 32127
- seq_lengths: int32 [8], replicated, may hold values from 1 to 2048, as said below
Outputs:
- log_probs: float32 [16384], P('width')
- entropies: float32 [16384], P('width')
Inputs may be any that keep to these rules, and one draw needn't show every extreme that they name: `seq_lengths`: each sequence has 1 to 2048 live tokens at its start; some sequence has exactly 2048.
All inputs are finite; a program needn't handle non-finite values.
Results may differ from a plain program's by a relative error of at most 0.0041.
Values may be sent and summed in bfloat16 or wider, within the bound.
A program may use at most 320 MiB of HBM per device.

v0:
```python
import jax
import jax.numpy as jnp
from jax import lax
from jax.sharding import PartitionSpec as P

D = 1024
SEQ_LEN = 2048


def on_device(hidden, norm_gain, head_weight, token_ids, seq_lengths):
    hidden_wide = hidden.astype(jnp.float32)
    square_part = jnp.sum(hidden_wide * hidden_wide, axis=1)
    square_sum = lax.psum(square_part, "width")
    normed = (hidden_wide * lax.rsqrt(square_sum / D + 1e-06)[:, None] * norm_gain[None, :]).astype(
        jnp.bfloat16
    )
    gathered = lax.all_gather(normed, "vocab", axis=0, tiled=True)
    width_count = lax.axis_size("width")
    row_count = gathered.shape[0] // width_count
    full_rows = lax.all_to_all(gathered, "width", split_axis=0, concat_axis=1, tiled=True)
    logits = jnp.dot(
        full_rows,
        lax.all_gather(head_weight, "width", axis=0, tiled=True),
        preferred_element_type=jnp.float32,
    )
    shard_columns = logits.shape[1]
    first_column = lax.axis_index("vocab") * shard_columns
    local_ids = token_ids - first_column
    target_hit = lax.broadcasted_iota(jnp.int32, logits.shape, 1) == local_ids[:, None]
    target = jnp.sum(jnp.where(target_hit, logits, 0.0), axis=1)
    largest = lax.pmax(jnp.max(logits, axis=1), "vocab")
    shifted = logits - largest[:, None]
    exponent_terms = jnp.exp(shifted)
    total_exp, weighted, target = lax.psum(
        (jnp.sum(exponent_terms, axis=1), jnp.sum(exponent_terms * shifted, axis=1), target),
        "vocab",
    )
    logsum = jnp.log(total_exp)
    log_probs = target - (largest + logsum)
    entropies = logsum - weighted / total_exp
    row_index = lax.axis_index("width") * row_count + lax.iota(jnp.int32, row_count)
    position = row_index % SEQ_LEN
    sequence = row_index // SEQ_LEN
    seq_match = sequence[:, None] == lax.iota(jnp.int32, seq_lengths.shape[0])[None, :]
    seq_limit = jnp.sum(jnp.where(seq_match, seq_lengths[None, :], 0), axis=1)
    live_rows = position < seq_limit
    return (jnp.where(live_rows, log_probs, 0.0), jnp.where(live_rows, entropies, 0.0))


def solution(mesh):
    in_specs = (P("vocab", "width"), P("width"), P("width", "vocab"), P("width"), P())
    out_specs = (P("width"), P("width"))
    return jax.shard_map(
        on_device, mesh=mesh, in_specs=in_specs, out_specs=out_specs, check_vma=False
    )
```

profile of v0, /device:TPU:0, one launch (start us, length us, event | category | flops | bytes accessed | tf_op | source)
XLA Modules:
  0.0 293.2 jit_solution(10053484098533443492)
XLA Ops:
  7.2 0.0 all-gather.3.cloned.1.call-start
  7.2 1.2 fusion.1
  8.4 15.0 %psum.28 = f32[1024]{0:T(1024)S(1)} all-reduce(f32[1024]{0:T(1024)S(1)} %fusion.1), channel_id=1, replica_groups=mesh['vocab'=16,'width'=8] {'width'}, use_global_device_ids=true, to_apply=%region_2.3 | all-reduce | flops 1024 | bytes 8192 | tf_op jit(solution)/shard_map/psum | solution.py:13
  23.4 1.8 fusion.3
  25.2 0.0 all-gather.3.cloned.1.call-update
  25.2 0.0 all-gather.5.cloned.1.call-start
  25.3 0.7 all-gather.5.cloned.1.call-update
  26.0 50.6 %all-gather.3.cloned.1.call-done = bf16[16384,128]{1,0:T(8,128)(2,1)} async-done(((bf16[1024,128]{1,0:T(8,128)(2,1)}), bf16[16384,128]{1,0:T(8,128)(2,1)}) %all-gather.3.cloned.1.call-update) | async-done | bytes 4194320 | tf_op jit(solution)/shard_map/all_gather | solution.py:17
  76.6 4.5 %all-to-all-start = ((bf16[8,2048,128]{2,1,0:T(8,128)(2,1)}), bf16[8,2048,128]{2,1,0:T(8,128)(2,1)}, u32[]{:S(2)}, u32[]{:S(2)}) async-start(bf16[8,2048,128]{2,1,0:T(8,128)(2,1)} %bitcast.5), calls=%async_computation | async-start | bytes 8388608 | tf_op jit(solution)/shard_map/all_to_all | solution.py:20
  81.2 0.7 select_reduce_fusion.1
  82.0 0.7 broadcast_subtract_fusion
  82.7 64.7 %all-to-all-done = bf16[8,2048,128]{2,1,0:T(8,128)(2,1)} async-done(((bf16[8,2048,128]{2,1,0:T(8,128)(2,1)}), bf16[8,2048,128]{2,1,0:T(8,128)(2,1)}, u32[]{:S(2)}, u32[]{:S(2)}) %all-to-all-start) | async-done | bytes 4194336 | tf_op jit(solution)/shard_map/all_to_all | solution.py:20
  147.3 6.5 %copy.8 = bf16[2048,8,128]{0,2,1:T(8,128)(2,1)} copy(bf16[2048,8,128]{2,0,1:T(8,128)(2,1)} %bitcast.1) | data formatting | bytes 8388608 | tf_op jit(solution)/shard_map/all_to_all | solution.py:20
  153.9 0.0 all-gather.5.cloned.1.call-done
  153.9 14.8 %fusion.10 = (f32[2048]{0:T(1024)S(1)}, f32[2048,2008]{0,1:T(8,128)}) fusion(bf16[2048,1024]{0,1:T(8,128)(2,1)} %bitcast.6, bf16[1024,2008]{0,1:T(8,128)(2,1)} %all-gather.5.cloned.1.call-done), kind=kOutput, calls=%fused_computation.29 | convolution fusion | flops 8426272768 | bytes 24764416 | tf_op jit(solution)/shard_map/dot_general | solution.py:21
  168.7 38.9 %pmax.7 = f32[2048]{0:T(1024)S(1)} all-reduce(f32[2048]{0:T(1024)S(1)} %get-tuple-element.10), channel_id=1, replica_groups=mesh['vocab'=16,'width'=8] {'vocab'}, use_global_device_ids=true, to_apply=%region_6.7 | all-reduce | flops 2048 | bytes 16384 | tf_op jit(solution)/shard_map/pmax | solution.py:31
  207.6 8.6 %fusion = (f32[2048]{0:T(1024)S(1)}, f32[2048]{0:T(1024)S(1)}, f32[2048]{0:T(1024)S(1)}) fusion(f32[2048,2008]{0,1:T(8,128)} %get-tuple-element.11, f32[2048]{0:T(1024)S(1)} %pmax.7, s32[2048]{0:T(1024)S(1)} %broadcast_subtract_fusion), kind=kLoop, calls=%fused_computation.2 | loop fusion | flops 28780544 | bytes 16490496 | tf_op jit(solution)/shard_map/reduce_sum | solution.py:35
  216.2 69.6 %all-reduce = (f32[2048]{0:T(1024)S(1)}, f32[2048]{0:T(1024)S(1)}, f32[2048]{0:T(1024)S(1)}) all-reduce(f32[2048]{0:T(1024)S(1)} %get-tuple-element.4, f32[2048]{0:T(1024)S(1)} %get-tuple-element.3, f32[2048]{0:T(1024)S(1)} %get-tuple-element.2), channel_id=1, replica_groups=mesh['vocab'=16,'width'=8] {'vocab'}, use_global_device_ids=true, to_apply=%region_4.5 | all-reduce | flops 6144 | bytes 49152 | tf_op jit(solution)/shard_map/psum | solution.py:34
  285.8 0.6 subtract_select_fusion
  (2 shorter events, 0.0 us)
Async XLA Ops:
  7.2 69.5 %all-gather.3.cloned.1.call-start = ((), (), s32[]{:S(2)}) async-start(), calls=%async_computation.1 | async-start | bytes 4456448 | tf_op jit(solution)/shard_map/all_gather | solution.py:17
  25.2 128.6 %all-gather.5.cloned.1.call-start = ((), (), s32[]{:S(2)}) async-start(), calls=%async_computation.2 | async-start | bytes 4626432 | tf_op jit(solution)/shard_map/all_gather | solution.py:23
  76.6 70.7 %all-to-all-start = ((bf16[8,2048,128]{2,1,0:T(8,128)(2,1)}), bf16[8,2048,128]{2,1,0:T(8,128)(2,1)}, u32[]{:S(2)}, u32[]{:S(2)}) async-start(bf16[8,2048,128]{2,1,0:T(8,128)(2,1)} %bitcast.5), calls=%async_computation | async-start | bytes 8388608 | tf_op jit(solution)/shard_map/all_to_all | solution.py:20
Sparse Core Ops, SparseCore 0:
  25.4 51.2 all-gather.2
  78.3 58.6 all-gather.4
where the time goes:
time: 294 us; the launch traced here: 293 us
  blocking collectives  123 us (42%)
  waiting for transfers between devices  116 us (39%)
  matrix products  14.8 us (5%)
  between operations  14.1 us (5%)
  other arithmetic  13.6 us (5%)
  local copies, waits for them, and re-layouts  6.52 us (2%)
  starting transfers between devices  4.63 us (2%)
    psum x1, blocking collectives, on_device(): lax.psum((jnp.sum(exponent_terms, axis=1), jnp.sum(exponent_terms * shift...  69.6 us
    all_to_all x1, waiting for transfers between devices, on_device(): lax.all_to_all(gathered, 'width', split_axis=0, concat_axis=1, tiled=True)  64.7 us
    all_gather x1, waiting for transfers between devices, on_device(): gathered = lax.all_gather(normed, 'vocab', axis=0, tiled=True)  50.6 us
    pmax x1, blocking collectives, on_device(): largest = lax.pmax(jnp.max(logits, axis=1), 'vocab')  38.9 us
    psum x1, blocking collectives, on_device(): square_sum = lax.psum(square_part, 'width')  15 us
    dot_general x1, matrix products, on_device(): jnp.dot(full_rows, lax.all_gather(head_weight, 'width', axis=0, tiled=Tru...  14.8 us
    reduce_sum x1, other arithmetic, on_device(): jnp.sum(exponent_terms * shifted, axis=1)  8.56 us
    all_to_all x1, local copies, waits for them, and re-layouts, on_device(): lax.all_to_all(gathered, 'width', split_axis=0, concat_axis=1, tiled=True)  6.52 us
  transfers between devices with their start and end apart: 3, of which 2 were waited for; matrix products, arithmetic and copies ran while one was open for 3% of the time, Pallas kernels for 0%

commit v1 on v0

v1 whole, which is shorter than its diff:
```python
import jax
import jax.numpy as jnp
from jax import lax
from jax.experimental import pallas as pl
from jax.experimental.pallas import tpu as pltpu
from jax.sharding import PartitionSpec as P

D = 1024
SEQ_LEN = 2048
SIDE = 4
GROUPS = 8
ROWS = 128
CHUNK = 512
NCHUNK = 4
TILE = 256
NEG = -1e30
MESH = pl.DeviceIdType.MESH
ORDER = [(0, 0), (0, 1), (0, 3), (1, 0), (3, 0), (1, 1), (1, 3), (3, 1), (3, 3),
         (0, 2), (2, 0), (1, 2), (3, 2), (2, 1), (2, 3), (2, 2)]
SLOT = {d: i for i, d in enumerate(ORDER)}
NTILE = 16 * ROWS // TILE
STEPS = [(p, j) for p in range(NTILE) for j in range(NCHUNK)]


def kernel(hid, head, gain, ids, lens, lp_ref, ent_ref,
           xin, xn, wb, hall, hlast, gb, idb, idl, m, s, u, t, lb0, lb1, st_tx, st_rx, o_tx, o_rx,
           as_, ar, gs, gr, is_, ir, xs, xr, ws, wr, wl, ss_, sr, os_, or_):
    v = lax.axis_index("vocab")
    w = lax.axis_index("width")
    z, x = v // SIDE, v % SIDE
    y, c = w // 2, w % 2
    columns = head.shape[1]

    def at(dz, dx):
        return (lax.rem(z + dz + SIDE, SIDE) * SIDE + lax.rem(x + dx + SIDE, SIDE), w)

    def up(dy, other=0):
        return (v, lax.rem(y + dy + SIDE, SIDE) * 2 + (1 - c if other else c))

    def group(d):
        return lax.rem(w + d, GROUPS)

    def remote(src, dst, send, recv, dev):
        return pltpu.make_async_remote_copy(src_ref=src, dst_ref=dst, send_sem=send, recv_sem=recv,
                                            device_id=dev, device_id_type=MESH)

    barrier = pltpu.get_barrier_semaphore()
    peers = [(v, group(d)) for d in range(1, GROUPS)] + [at(0, 1), at(0, -1), at(1, 0), at(-1, 0)]
    for dev in peers:
        pl.semaphore_signal(barrier, inc=1, device_id=dev, device_id_type=MESH)
    pl.semaphore_wait(barrier, len(peers))

    sent = []

    def go(copy):
        copy.start()
        sent.append(copy)

    a_copies, g_copies, i_copies = [], [], []
    for d in (2, 3, 4, 5, 6, 7, 1):
        g = group(d)
        rows = pl.ds(pl.multiple_of(g * ROWS, ROWS), ROWS)
        a_copies.append(remote(hid.at[rows, :], xin.at[w], as_.at[d], ar.at[d], (v, g)))
        g_copies.append(remote(gain, gb.at[w], gs.at[d], gr.at[d], (v, g)))
        i_copies.append(remote(ids.at[:, g], idb.at[w], is_.at[d], ir.at[d], (v, g)))
    own_rows = pl.ds(pl.multiple_of(w * ROWS, ROWS), ROWS)
    local = [pltpu.make_async_copy(hid.at[own_rows, :], xin.at[w], as_.at[0]),
             pltpu.make_async_copy(gain, gb.at[w], gs.at[0]),
             pltpu.make_async_copy(ids.at[:, w], idb.at[w], is_.at[0])]
    for copy in a_copies + g_copies + i_copies:
        go(copy)
    for copy in local:
        copy.start()
    whole = pltpu.make_async_copy(head, hall, wl.at[NCHUNK])
    whole.start()

    def wrows(dy, lo=0, n=ROWS):
        src = lax.rem(y - dy + SIDE, SIDE) * 2 + c
        return pl.ds(pl.multiple_of(src * ROWS + lo, 64), n)

    W = {}
    wlocal = {}
    for j in range(NCHUNK):
        mine = head.at[:, pl.ds(j * CHUNK, CHUNK)] if j < NCHUNK - 1 else hlast

        def wv(rows):
            return wb.at[j, rows, :]

        def wcopy(k, src, dst, dev):
            W[j, k] = remote(src, dst, ws.at[j * 9 + k], wr.at[j * 9 + k], dev)

        wcopy(0, mine, wv(wrows(0)), up(1))
        wcopy(1, mine, wv(wrows(0)), up(-1))
        wcopy(2, mine, wv(wrows(0)), up(0, 1))
        wcopy(3, wv(wrows(1, 0, 64)), wv(wrows(1, 0, 64)), up(1))
        wcopy(4, wv(wrows(1)), wv(wrows(1)), up(0, 1))
        wcopy(5, wv(wrows(3, 64, 64)), wv(wrows(3, 64, 64)), up(-1))
        wcopy(6, wv(wrows(3)), wv(wrows(3)), up(0, 1))
        wcopy(7, wv(wrows(2, 0, 64)), wv(wrows(2, 0, 64)), up(0, 1))
        wcopy(8, wv(wrows(2, 64, 64)), wv(wrows(2, 64, 64)), up(0, 1))
        wlocal[j] = pltpu.make_async_copy(mine, wv(wrows(0)), wl.at[j])

    def w_own(j):
        wlocal[j].start()
        for k in (0, 1, 2):
            go(W[j, k])

    def w_forward(j):
        W[j, 0].wait_recv()
        go(W[j, 3])
        go(W[j, 4])
        W[j, 1].wait_recv()
        go(W[j, 5])
        go(W[j, 6])

    def w_across(j):
        W[j, 3].wait_recv()
        go(W[j, 7])
        W[j, 5].wait_recv()
        go(W[j, 8])

    def w_done(j):
        wlocal[j].wait()
        for k in (2, 4, 6, 7, 8):
            W[j, k].wait_recv()

    X = {}

    def xcopy(name, d, lo, n, az, ax):
        to = ((d[0] + az) % SIDE, (d[1] + ax) % SIDE)
        k = len(X)
        X[name] = remote(xn.at[SLOT[d], pl.ds(lo, n), :], xn.at[SLOT[to], pl.ds(lo, n), :],
                         xs.at[k], xr.at[k], at(az, ax))

    def turn(h, a, b):
        return (b, a) if h == 0 else (a, b)

    for h in (0, 1):
        lo = 64 * h
        for sgn, near in ((1, 1), (-1, 3)):
            q = lo if sgn == 1 else lo + 32
            xcopy((h, "first", near), (0, 0), lo, 64, *turn(h, sgn, 0))
            xcopy((h, "first", 2, near), turn(h, near, 0), q, 32, *turn(h, sgn, 0))
            for far in range(SIDE):
                xcopy((h, "second", far, near), turn(h, far, 0), lo, 64, *turn(h, 0, sgn))
                xcopy((h, "last", far, near), turn(h, far, near), q, 32, *turn(h, 0, sgn))

    def x_own():
        for h in (0, 1):
            for near in (1, 3):
                go(X[h, "first", near])
        for h in (0, 1):
            for near in (1, 3):
                go(X[h, "second", 0, near])

    def x_round1():
        for h in (0, 1):
            for near in (1, 3):
                X[h, "first", near].wait_recv()
                go(X[h, "first", 2, near])
                for side in (1, 3):
                    go(X[h, "second", near, side])

    def x_round2():
        for h in (0, 1):
            for near in (1, 3):
                X[h, "second", 0, near].wait_recv()
                go(X[h, "last", 0, near])

    def x_round3():
        for h in (0, 1):
            for near in (1, 3):
                X[h, "first", 2, near].wait_recv()
            for side in (1, 3):
                go(X[h, "second", 2, side])

    def x_round4():
        for h in (0, 1):
            for far in (1, 3):
                for near in (1, 3):
                    X[h, "second", far, near].wait_recv()
                    go(X[h, "last", far, near])

    def x_round5():
        for h in (0, 1):
            for near in (1, 3):
                X[h, "second", 2, near].wait_recv()
                go(X[h, "last", 2, near])

    def x_tail():
        for h in (0, 1):
            for far in range(SIDE):
                for near in (1, 3):
                    X[h, "last", far, near].wait_recv()

    w_own(0)
    w_own(1)

    m[...] = jnp.full(m.shape, NEG, jnp.float32)
    for ref in (s, u, t):
        ref[...] = jnp.zeros(ref.shape, jnp.float32)

    for copy in local[:2]:
        copy.wait()
    for copy in a_copies + g_copies:
        copy.wait_recv()
    for r in range(0, ROWS, 32):
        wide = [xin[k, r:r + 32, :].astype(jnp.float32) for k in range(GROUPS)]
        squares = wide[0] * wide[0]
        for k in range(1, GROUPS):
            squares = squares + wide[k] * wide[k]
        scale = lax.rsqrt(jnp.sum(squares, axis=1, keepdims=True) / D + 1e-06)
        for k in range(GROUPS):
            xn[0, r:r + 32, k * 128:(k + 1) * 128] = (wide[k] * scale * gb[k]).astype(jnp.bfloat16)
    x_own()

    whole.wait()
    first = (NCHUNK - 1) * CHUNK
    hlast[:, (columns - first) // 128 * 128:] = jnp.zeros((ROWS, CHUNK - (columns - first) // 128 * 128), jnp.bfloat16)
    hlast[:, 0:columns - first] = hall[:, first:columns]

    local[2].wait()
    for copy in i_copies:
        copy.wait_recv()
    lane = lax.broadcasted_iota(jnp.int32, (ROWS, 128), 1)
    base = v * columns
    for q, (dz, dx) in enumerate(ORDER):
        block = lax.rem(z - dz + SIDE, SIDE) * SIDE + lax.rem(x - dx + SIDE, SIDE)
        row = idb[block // 2, block % 2]
        row = jnp.where(row - base < columns, row - base, -1)
        idl[q * ROWS:(q + 1) * ROWS, :] = jnp.broadcast_to(row, (ROWS, 128)).T - lane

    w_forward(0)
    w_own(2)
    x_round1()
    w_across(0)
    w_forward(1)
    w_own(3)
    x_round2()
    x_round3()
    w_across(1)
    w_forward(2)
    x_round4()
    w_across(2)
    w_forward(3)
    x_round5()
    w_across(3)
    for j in range(NCHUNK):
        w_done(j)
    x_tail()

    def pick(values, i):
        out = jnp.int32(values[0])
        for k in range(1, len(values)):
            out = jnp.where(i >= k, jnp.int32(values[k]), out)
        return out

    def tile_of(i):
        return i // NCHUNK, i % NCHUNK

    def dot(i, buf):
        p, j = tile_of(i)
        lhs = jnp.concatenate([xn[p * 2], xn[p * 2 + 1]], axis=0)
        buf[...] = jnp.dot(lhs, wb[j], preferred_element_type=jnp.float32)

    group_rows = 16
    parts = CHUNK // 128
    lane_g = lax.broadcasted_iota(jnp.int32, (group_rows, 128), 1)

    def stats(i, buf):
        p, j = tile_of(i)
        row0 = p * TILE
        col0 = j * CHUNK
        edge = lane_g < columns - (parts - 1) * 128 - col0
        for g in range(TILE // group_rows):
            rows = pl.ds(pl.multiple_of(row0 + g * group_rows, group_rows), group_rows)
            ls = [buf[g * group_rows:(g + 1) * group_rows, k * 128:(k + 1) * 128] for k in range(parts)]
            ls[-1] = jnp.where(edge, ls[-1], NEG)
            m_old = m[rows, :]
            top = jnp.maximum(jnp.maximum(ls[0], ls[1]), jnp.maximum(ls[2], ls[3]))
            m_new = jnp.maximum(m_old, top)
            fade = jnp.exp(m_old - m_new)
            s_new = s[rows, :] * fade
            u_new = u[rows, :] * fade
            t_new = t[rows, :]
            here = idl[rows, :]
            for k in range(parts):
                e = jnp.exp(ls[k] - m_new)
                s_new = s_new + e
                u_new = u_new + e * ls[k]
                t_new = jnp.where(here == col0 + k * 128, ls[k], t_new)
            m[rows, :] = m_new
            s[rows, :] = s_new
            u[rows, :] = u_new
            t[rows, :] = t_new

    total = len(STEPS)
    dot(0, lb0)

    @pl.loop(0, total // 2)
    def _(h):
        i = h * 2
        dot(i + 1, lb1)
        stats(i, lb0)
        dot(jnp.minimum(i + 2, total - 1), lb0)
        stats(i + 1, lb1)

    @pl.loop(0, 16)
    def _(q):
        rows = pl.ds(pl.multiple_of(q * ROWS, ROWS), ROWS)
        mt = m[rows, :].T
        peak = jnp.max(mt, axis=0, keepdims=True)
        scale = jnp.exp(mt - peak)
        st_tx[q, 0:1, :] = peak
        st_tx[q, 1:2, :] = jnp.sum(s[rows, :].T * scale, axis=0, keepdims=True)
        st_tx[q, 2:3, :] = jnp.sum(u[rows, :].T * scale, axis=0, keepdims=True)
        st_tx[q, 3:4, :] = jnp.sum(t[rows, :].T, axis=0, keepdims=True)

    S = []
    for q in range(1, 16):
        dz, dx = ORDER[q]
        S.append(remote(st_tx.at[q], st_rx.at[q], ss_.at[q], sr.at[q], at(-dz, -dx)))
        go(S[-1])
    for copy in S:
        copy.wait_recv()

    stat = [st_tx[0]] + [st_rx[q] for q in range(1, 16)]
    peak = stat[0][0:1, :]
    for a in stat[1:]:
        peak = jnp.maximum(peak, a[0:1, :])
    sum_e = jnp.zeros_like(peak)
    sum_w = jnp.zeros_like(peak)
    target = jnp.zeros_like(peak)
    for a in stat:
        f = jnp.exp(a[0:1, :] - peak)
        sum_e = sum_e + a[1:2, :] * f
        sum_w = sum_w + a[2:3, :] * f
        target = target + a[3:4, :]
    log_total = peak + jnp.log(sum_e)
    position = lax.rem(v, 2) * (SEQ_LEN // 2) + w * ROWS + lax.broadcasted_iota(jnp.int32, (1, 128), 1)
    live = position < lens[v // 2]
    o_tx[0:1, :] = jnp.where(live, target - log_total, 0.0)
    o_tx[1:2, :] = jnp.where(live, log_total - sum_w / sum_e, 0.0)

    goal = v // 2
    mine = lax.rem(v, 2) * GROUPS + w
    for k in range(16):
        copy = remote(o_tx, o_rx.at[mine], os_.at[k], or_.at[mine], (k, goal))

        @pl.when(jnp.logical_not(jnp.logical_and(k == v, goal == w)))
        def _():
            copy.start()

    @pl.when(goal == w)
    def _():
        o_rx[mine] = o_tx[...]

    for k in range(16):
        copy = remote(o_tx, o_rx.at[k], os_.at[k], or_.at[k], (v, w))

        @pl.when(jnp.logical_not(jnp.logical_and(2 * w + k // GROUPS == v, k % GROUPS == w)))
        def _():
            copy.wait_recv()

        @pl.when(jnp.logical_not(jnp.logical_and(k == v, goal == w)))
        def _():
            copy.wait_send()

    for k in range(16):
        lp_ref[k:k + 1, :] = o_rx[k, 0:1, :]
        ent_ref[k:k + 1, :] = o_rx[k, 1:2, :]
    for copy in sent:
        copy.wait_send()


def on_device(hidden, norm_gain, head_weight, token_ids, seq_lengths):
    hbm = pl.BlockSpec(memory_space=pl.ANY)
    vmem = pl.BlockSpec(memory_space=pltpu.VMEM)
    smem = pl.BlockSpec(memory_space=pltpu.SMEM)
    f32, bf16, i32 = jnp.float32, jnp.bfloat16, jnp.int32
    dma = pltpu.SemaphoreType.DMA
    lp, ent = pl.pallas_call(
        kernel,
        out_shape=(jax.ShapeDtypeStruct((16, 128), f32), jax.ShapeDtypeStruct((16, 128), f32)),
        in_specs=[hbm, hbm, hbm, hbm, smem],
        out_specs=(vmem, vmem),
        scratch_shapes=[
            pltpu.VMEM((GROUPS, ROWS, 128), bf16),
            pltpu.VMEM((16, ROWS, D), bf16),
            pltpu.VMEM((NCHUNK, D, CHUNK), bf16),
            pltpu.VMEM(head_weight.shape, bf16),
            pltpu.VMEM((ROWS, CHUNK), bf16),
            pltpu.VMEM((GROUPS, 1, 128), f32),
            pltpu.VMEM((GROUPS, 2, 1, 128), i32),
            pltpu.VMEM((16 * ROWS, 128), i32),
            pltpu.VMEM((16 * ROWS, 128), f32),
            pltpu.VMEM((16 * ROWS, 128), f32),
            pltpu.VMEM((16 * ROWS, 128), f32),
            pltpu.VMEM((16 * ROWS, 128), f32),
            pltpu.VMEM((TILE, CHUNK), f32),
            pltpu.VMEM((TILE, CHUNK), f32),
            pltpu.VMEM((16, 4, 128), f32),
            pltpu.VMEM((16, 4, 128), f32),
            pltpu.VMEM((2, 128), f32),
            pltpu.VMEM((16, 2, 128), f32),
            dma((8,)), dma((8,)), dma((8,)), dma((8,)), dma((8,)), dma((8,)),
            dma((40,)), dma((40,)), dma((36,)), dma((36,)), dma((5,)),
            dma((16,)), dma((16,)), dma((16,)), dma((16,)),
        ],
        compiler_params=pltpu.CompilerParams(
            collective_id=0, has_side_effects=True, vmem_limit_bytes=56 * 2**20),
        name="score",
    )(hidden, head_weight, norm_gain.reshape(1, 128), token_ids.reshape(2, GROUPS, 1, 128), seq_lengths)
    return lp.reshape(2048), ent.reshape(2048)


def solution(mesh):
    in_specs = (P("vocab", "width"), P("width"), P("width", "vocab"), P("width"), P())
    out_specs = (P("width"), P("width"))
    return jax.shard_map(
        on_device, mesh=mesh, in_specs=in_specs, out_specs=out_specs, check_vma=False
    )
```

time: 294 us -> 71.2 us (0.24)
  the two profiles are of different devices: /device:TPU:0 before, /device:TPU:1 now
where the time goes in v1:
time: 71.2 us; the launch traced here: 71 us
  Pallas kernels  66.4 us (93%)
  local copies, waits for them, and re-layouts  3.96 us (6%)
    pallas_call x1, Pallas kernels, on_device(): pl.pallas_call(kernel, out_shape=(jax.ShapeDtypeStruct((16, 128), f32), j...  66.4 us
    unnamed x5, local copies, waits for them, and re-layouts  3.96 us

profile of v1, /device:TPU:1, one launch (start us, length us, event | category | flops | bytes accessed | tf_op | source)
XLA Modules:
  0.0 71.0 jit_solution(12240165362846890761)
XLA Ops:
  0.6 2.1 %copy.7.head = bf16[128,2008]{1,0:T(8,128)(2,1)} copy(bf16[128,2008]{0,1:T(8,128)(2,1)} %param.7) | data formatting | bytes 1028096 | tf_op args[2]
  2.7 66.4 %score.1 = (f32[16,128]{1,0:T(8,128)}, f32[16,128]{1,0:T(8,128)}) custom-call(bf16[1024,128]{1,0:T(8,128)(2,1)} %hid.1, bf16[128,2008]{1,0:T(8,128)(2,1)} %copy.7.head, f32[1,128]{1,0:T(1,128)} %bitcast.7, s32[2,8,1,128]{3,2,1,0:T(1,128)} %bitcast.4, s32[8]{0:T(128)} %lens.1), custom_call_target="tpu_custom_call" | custom-call | tf_op jit(solution)/shard_map/score/pallas_call | solution.py:382
  69.1 0.0 copy-start
  69.1 1.3 %copy.10 = f32[2048]{0:T(1024)} copy(f32[2048]{0:T(1024)} %bitcast.6) | data formatting | bytes 16384
  70.4 0.0 copy-done
  70.4 0.6 copy.11
Async XLA Ops:
  69.1 1.3 %copy-start = (f32[16,128]{1,0:T(8,128)S(1)}, f32[16,128]{1,0:T(8,128)}, u32[]{:S(2)}) copy-start(f32[16,128]{1,0:T(8,128)} %get-tuple-element.5) | copy-start | bytes 24580

commit v2 on v1

v2 whole, which is shorter than its diff:
```python
import jax
import jax.numpy as jnp
from jax import lax
from jax.experimental import pallas as pl
from jax.experimental.pallas import tpu as pltpu
from jax.sharding import PartitionSpec as P

D = 1024
SEQ_LEN = 2048
SEQS = 8
SIDE = 4
GROUPS = 8
ROWS = 128
HALF = 64
CHUNK = 512
NCHUNK = 4
TILE = 256
NEG = -1e30
MESH = pl.DeviceIdType.MESH
UNITS = [(0, 0, 0), (1, 0, 0), (0, 0, 1), (1, 1, 0),
         (0, 0, 3), (1, 3, 0), (0, 1, 0), (1, 0, 1),
         (0, 3, 0), (1, 0, 3), (0, 0, 2), (1, 2, 0),
         (0, 1, 1), (1, 1, 1), (0, 3, 1), (1, 1, 3),
         (0, 1, 3), (1, 3, 1), (0, 3, 3), (1, 3, 3),
         (0, 2, 0), (1, 0, 2), (0, 1, 2), (1, 2, 1),
         (0, 3, 2), (1, 2, 3), (0, 2, 1), (1, 1, 2),
         (0, 2, 3), (1, 3, 2), (0, 2, 2), (1, 2, 2)]
PLACE = {d: i for i, d in enumerate(UNITS)}
NTILE = 8
STEPS = [(0, 0), (1, 0), (2, 0), (0, 1), (1, 1), (2, 1), (3, 0), (3, 1),
         (0, 2), (1, 2), (2, 2), (3, 2), (4, 0), (4, 1), (4, 2), (4, 3),
         (3, 3), (2, 3), (5, 0), (5, 1), (5, 2), (5, 3), (6, 0), (6, 1),
         (6, 2), (6, 3), (7, 0), (7, 1), (7, 2), (7, 3), (1, 3), (0, 3)]
PART = 256
NPART = 8


def kernel(hid, head, gain, ids, lens, out,
           xin, xn, wb, aux, idl, m, s, u, t, lb0, lb1, st_tx, st_rx, o_tx, lens_v, gain_v, ids_v, aux_tx,
           as_, ar, gs, gr, is_, xs, xr, ws, wr, wl, ss_, sr, os_, or_, ls_):
    v = lax.axis_index("vocab")
    w = lax.axis_index("width")
    z, x = v // SIDE, v % SIDE
    y, c = w // 2, w % 2
    columns = head.shape[0]

    def at(dz, dx):
        return (lax.rem(z + dz + SIDE, SIDE) * SIDE + lax.rem(x + dx + SIDE, SIDE), w)

    def up(dy, other=0):
        return (v, lax.rem(y + dy + SIDE, SIDE) * 2 + (1 - c if other else c))

    def group(d):
        return lax.rem(w + d, GROUPS)

    def remote(src, dst, send, recv, dev):
        return pltpu.make_async_remote_copy(src_ref=src, dst_ref=dst, send_sem=send, recv_sem=recv,
                                            device_id=dev, device_id_type=MESH)

    barrier = pltpu.get_barrier_semaphore()
    peers = [(v, group(d)) for d in range(1, GROUPS)] + [at(0, 1), at(0, -1), at(1, 0), at(-1, 0)]
    for dev in peers:
        pl.semaphore_signal(barrier, inc=1, device_id=dev, device_id_type=MESH)
    own_gain = pltpu.make_async_copy(gain, gain_v, gs.at[0])
    own_ids = pltpu.make_async_copy(ids, ids_v, is_.at[0])
    lens_copy = pltpu.make_async_copy(lens, lens_v, ls_.at[0])
    for copy in (own_gain, own_ids, lens_copy):
        copy.start()
    for copy in (own_gain, own_ids, lens_copy):
        copy.wait()
    for g in range(GROUPS):
        for k in (0, 1):
            aux_tx[g, k:k + 1, :] = ids_v[k, g].astype(jnp.float32)
        aux_tx[g, 2:3, :] = gain_v[...]
    pl.semaphore_wait(barrier, len(peers))

    sent = []

    def go(copy):
        copy.start()
        sent.append(copy)

    a_copies, g_copies = {0: [], 1: []}, []
    own = []
    for h in (0, 1):
        for d in range(GROUPS):
            g = group(d)
            rows = pl.ds(pl.multiple_of(g * ROWS + h * HALF, HALF), HALF)
            place = xin.at[w, pl.ds(h * HALF, HALF), :]
            if d == 0:
                own.append(pltpu.make_async_copy(hid.at[rows, :], place, as_.at[h, 0]))
            else:
                a_copies[h].append(remote(hid.at[rows, :], place, as_.at[h, d], ar.at[h, d], (v, g)))
    for d in range(1, GROUPS):
        g = group(d)
        g_copies.append(remote(aux_tx.at[g], aux.at[w], gs.at[d], gr.at[d], (v, g)))
    def wcols(dy):
        src = lax.rem(y - dy + SIDE, SIDE) * 2 + c
        return pl.ds(pl.multiple_of(src * 128, 128), 128)

    W = {}
    wlocal = {}
    for j in range(NPART):
        n = min(PART, columns - j * PART)
        mine = head.at[pl.ds(j * PART, n), :]
        mid = PART // 2
        row0 = j % 2 * PART

        def wv(dy, lo=0, hi=n):
            return wb.at[j // 2, pl.ds(row0 + lo, hi - lo), wcols(dy)]

        def wcopy(k, src, dst, dev):
            W[j, k] = remote(src, dst, ws.at[j * 9 + k], wr.at[j * 9 + k], dev)

        wcopy(0, mine, wv(0), up(1))
        wcopy(1, mine, wv(0), up(-1))
        wcopy(2, mine, wv(0), up(0, 1))
        wcopy(3, wv(1, 0, mid), wv(1, 0, mid), up(1))
        wcopy(4, wv(1), wv(1), up(0, 1))
        wcopy(5, wv(3, mid), wv(3, mid), up(-1))
        wcopy(6, wv(3), wv(3), up(0, 1))
        wcopy(7, wv(2, 0, mid), wv(2, 0, mid), up(0, 1))
        wcopy(8, wv(2, mid), wv(2, mid), up(0, 1))
        wlocal[j] = pltpu.make_async_copy(mine, wv(0), wl.at[j])

    def w_own(j):
        for k in (0, 1, 2):
            go(W[j, k])
        wlocal[j].start()

    def w_forward(j):
        W[j, 0].wait_recv()
        go(W[j, 3])
        W[j, 1].wait_recv()
        go(W[j, 5])
        go(W[j, 4])
        go(W[j, 6])

    def w_across(j):
        W[j, 3].wait_recv()
        go(W[j, 7])
        W[j, 5].wait_recv()
        go(W[j, 8])

    def w_done(chunk):
        for j in (2 * chunk, 2 * chunk + 1):
            wlocal[j].wait()
            for k in (2, 4, 6, 7, 8):
                W[j, k].wait_recv()

    X = {}

    def turn(h, a, b):
        return (b, a) if h == 0 else (a, b)

    def xcopy(name, h, d, lo, n, step):
        to = ((d[0] + step[0]) % SIDE, (d[1] + step[1]) % SIDE)
        k = len(X)
        X[name] = remote(xn.at[PLACE[h, *d], pl.ds(lo, n), :], xn.at[PLACE[h, *to], pl.ds(lo, n), :],
                         xs.at[k], xr.at[k], at(*step))

    for h in (0, 1):
        for sgn, near in ((1, 1), (-1, 3)):
            q = 0 if sgn == 1 else 32
            xcopy((h, "first", near), h, (0, 0), 0, 64, turn(h, sgn, 0))
            xcopy((h, "first", 2, near), h, turn(h, near, 0), q, 32, turn(h, sgn, 0))
            for far in range(SIDE):
                xcopy((h, "second", far, near), h, turn(h, far, 0), 0, 64, turn(h, 0, sgn))
                xcopy((h, "last", far, near), h, turn(h, far, near), q, 32, turn(h, 0, sgn))

    def x_own(h):
        for near in (1, 3):
            go(X[h, "first", near])

    def x_own_across():
        for h in (0, 1):
            for near in (1, 3):
                go(X[h, "second", 0, near])

    def x_round1():
        for h in (0, 1):
            for near in (1, 3):
                X[h, "first", near].wait_recv()
                go(X[h, "first", 2, near])

    def x_near(near):
        for h in (0, 1):
            for side in (1, 3):
                go(X[h, "second", near, side])

    def x_pace():
        for h in (0, 1):
            for near in (1, 3):
                X[h, "second", 0, near].wait_recv()

    def x_round2():
        for h in (0, 1):
            for near in (1, 3):
                go(X[h, "last", 0, near])

    def x_round3_wait():
        for h in (0, 1):
            for near in (1, 3):
                X[h, "first", 2, near].wait_recv()

    def x_round3():
        for h in (0, 1):
            for side in (1, 3):
                go(X[h, "second", 2, side])

    def x_round4(far):
        for h in (0, 1):
            for near in (1, 3):
                X[h, "second", far, near].wait_recv()
                go(X[h, "last", far, near])

    def x_round5():
        for h in (0, 1):
            for near in (1, 3):
                X[h, "second", 2, near].wait_recv()
                go(X[h, "last", 2, near])

    def x_last(far):
        for h in (0, 1):
            for near in (1, 3):
                X[h, "last", far, near].wait_recv()

    far_first = (3, 4, 2, 5, 1, 6, 0)
    for k in far_first:
        go(a_copies[0][k])
    w_own(0)
    for copy in g_copies:
        go(copy)
    for k in far_first:
        go(a_copies[1][k])
    w_own(1)
    for copy in own:
        copy.start()
    aux[w] = aux_tx[w]

    m[...] = jnp.full(m.shape, NEG, jnp.float32)
    for ref in (s, u, t):
        ref[...] = jnp.zeros(ref.shape, jnp.float32)

    w_forward(0)
    w_own(2)

    for h in (0, 1):
        own[h].wait()
        for copy in a_copies[h]:
            copy.wait_recv()
        if h == 0:
            for copy in g_copies:
                copy.wait_recv()
        for r in range(0, HALF, 32):
            wide = [xin[k, h * HALF + r:h * HALF + r + 32, :].astype(jnp.float32) for k in range(GROUPS)]
            squares = wide[0] * wide[0]
            for k in range(1, GROUPS):
                squares = squares + wide[k] * wide[k]
            scale = lax.rsqrt(jnp.sum(squares, axis=1, keepdims=True) / D + 1e-06)
            for k in range(GROUPS):
                xn[h, r:r + 32, k * 128:(k + 1) * 128] = (wide[k] * scale * aux[k, 2:3, :]).astype(jnp.bfloat16)
        x_own(h)
        if h == 0:
            w_own(3)

    w_across(0)
    x_own_across()

    which = lax.broadcasted_iota(jnp.int32, (1, SEQS), 1) == v // 2
    limit = jnp.sum(jnp.where(which, lens_v[...], 0), axis=1, keepdims=True)

    lane = lax.broadcasted_iota(jnp.int32, (ROWS, 128), 1)
    base = v * columns
    for dz in range(SIDE):
        for dx in range(SIDE):
            block = lax.rem(z - dz + SIDE, SIDE) * SIDE + lax.rem(x - dx + SIDE, SIDE)
            row = aux[block // 2, pl.ds(block % 2, 1), :].astype(jnp.int32)
            row = jnp.where(row - base < columns, row - base, -1)
            wide = jnp.broadcast_to(row, (ROWS, 128)).T - lane
            for h in (0, 1):
                idl[PLACE[h, dz, dx]] = wide[h * HALF:(h + 1) * HALF, :]

    w_forward(1)
    w_own(4)
    x_round1()
    x_near(1)
    w_across(1)
    w_forward(2)
    w_own(5)
    w_done(0)

    def pick(values, i):
        out = jnp.int32(values[0])
        for k in range(1, len(values)):
            if values[k] != values[k - 1]:
                out = jnp.where(i >= k, jnp.int32(values[k]), out)
        return out

    def tile_of(i):
        return pick([p for p, _ in STEPS], i), pick([j for _, j in STEPS], i)

    def dot(i, buf):
        p, j = tile_of(i)
        lhs = xn[pl.ds(p * 4, 4)].reshape(TILE, D)
        buf[...] = lax.dot_general(lhs, wb[j], (((1,), (1,)), ((), ())), preferred_element_type=jnp.float32)

    group_rows = 16
    parts = CHUNK // 128
    lane_g = lax.broadcasted_iota(jnp.int32, (group_rows, 128), 1)

    def stats(i, buf):
        p, j = tile_of(i)
        col0 = j * CHUNK
        edge = lane_g < columns - (parts - 1) * 128 - col0
        for g in range(TILE // group_rows):
            at_rows = (p * 4 + g * group_rows // HALF, pl.ds(g * group_rows % HALF, group_rows))
            ls = [buf[g * group_rows:(g + 1) * group_rows, k * 128:(k + 1) * 128] for k in range(parts)]
            ls[-1] = jnp.where(edge, ls[-1], NEG)
            m_old = m[at_rows]
            top = jnp.maximum(jnp.maximum(ls[0], ls[1]), jnp.maximum(ls[2], ls[3]))
            m_new = jnp.maximum(m_old, top)
            fade = jnp.exp(m_old - m_new)
            s_new = s[at_rows] * fade
            u_new = u[at_rows] * fade
            t_new = t[at_rows]
            here = idl[at_rows]
            for k in range(parts):
                e = jnp.exp(ls[k] - m_new)
                s_new = s_new + e
                u_new = u_new + e * ls[k]
                t_new = jnp.where(here == col0 + k * 128, ls[k], t_new)
            m[at_rows] = m_new
            s[at_rows] = s_new
            u[at_rows] = u_new
            t[at_rows] = t_new

    def finish(q):
        def rows_of(ref):
            return ref[pl.ds(q * 2, 2)].reshape(ROWS, 128).T

        mt = rows_of(m)
        peak = jnp.max(mt, axis=0, keepdims=True)
        scale = jnp.exp(mt - peak)
        st_tx[q, 0:1, :] = peak
        st_tx[q, 1:2, :] = jnp.sum(rows_of(s) * scale, axis=0, keepdims=True)
        st_tx[q, 2:3, :] = jnp.sum(rows_of(u) * scale, axis=0, keepdims=True)
        st_tx[q, 3:4, :] = jnp.sum(rows_of(t), axis=0, keepdims=True)

    S = {}
    for k, (h, dz, dx) in enumerate(UNITS):
        if k >= 2 and not (k % 2 == 1 and UNITS[k - 1][1:] == (dz, dx)):
            S[k] = remote(st_tx.at[k // 2], st_rx.at[k], ss_.at[k], sr.at[k], at(-dz, -dx))

    def send_stats(tile):
        for k in range(tile * 4, tile * 4 + 4):
            if k in S:
                go(S[k])

    def finish_tile(tile):
        finish(tile * 2)
        finish(tile * 2 + 1)
        send_stats(tile)

    def acts_0():
        w_forward(3)
        w_own(6)
        x_near(3)
        x_pace()
        w_across(2)
        x_round2()
        w_forward(4)
        w_own(7)
        x_round3_wait()
        x_round3()

    def acts_1():
        w_across(3)
        w_forward(5)
        w_done(1)

    def acts_2():
        w_across(4)
        x_round4(1)
        w_forward(6)

    def acts_3():
        w_across(5)
        w_forward(7)
        w_done(2)

    def acts_4():
        x_round4(3)

    def acts_5():
        w_across(6)

    def acts_6():
        w_across(7)
        x_round5()

    def acts_7():
        w_done(3)

    def acts_8():
        x_last(0)
        finish_tile(4)

    def acts_9():
        finish_tile(3)
        finish_tile(2)

    def acts_10():
        x_last(1)

    def acts_11():
        finish_tile(5)

    def acts_12():
        x_last(3)
        x_last(2)

    def acts_13():
        finish_tile(6)

    def acts_15():
        finish_tile(7)

    ACTS = {0: acts_0, 1: acts_1, 2: acts_2, 3: acts_3, 4: acts_4, 5: acts_5, 6: acts_6, 7: acts_7, 8: acts_8,
            9: acts_9, 10: acts_10, 11: acts_11, 12: acts_12, 13: acts_13, 15: acts_15}
    total = len(STEPS)
    dot(0, lb0)

    @pl.loop(0, total // 2)
    def _(h):
        i = h * 2
        for k in ACTS:
            pl.when(h == k)(ACTS[k])
        dot(i + 1, lb1)
        stats(i, lb0)
        dot(jnp.minimum(i + 2, total - 1), lb0)
        stats(i + 1, lb1)

    for tile in (1, 0):
        finish_tile(tile)
    for copy in S.values():
        copy.wait_recv()

    first_half = lax.broadcasted_iota(jnp.int32, (4, 128), 1) < HALF

    def stat_of(dz, dx):
        if (dz, dx) == (0, 0):
            return st_tx[0]
        a, b = PLACE[0, dz, dx], PLACE[1, dz, dx]
        if b not in S:
            return st_rx[a]
        return jnp.where(first_half, st_rx[a], st_rx[b])

    stat = [stat_of(dz, dx) for dz in range(SIDE) for dx in range(SIDE)]
    peak = stat[0][0:1, :]
    for a in stat[1:]:
        peak = jnp.maximum(peak, a[0:1, :])
    sum_e = jnp.zeros_like(peak)
    sum_w = jnp.zeros_like(peak)
    target = jnp.zeros_like(peak)
    for a in stat:
        f = jnp.exp(a[0:1, :] - peak)
        sum_e = sum_e + a[1:2, :] * f
        sum_w = sum_w + a[2:3, :] * f
        target = target + a[3:4, :]
    log_total = peak + jnp.log(sum_e)
    position = lax.rem(v, 2) * (SEQ_LEN // 2) + w * ROWS + lax.broadcasted_iota(jnp.int32, (1, 128), 1)
    live = position < limit
    o_tx[0] = jnp.where(live, target - log_total, 0.0)
    o_tx[1] = jnp.where(live, log_total - sum_w / sum_e, 0.0)

    goal = v // 2
    mine = lax.rem(v, 2) * GROUPS + w

    def result(k, place, dev):
        return remote(o_tx, out.at[:, place], os_.at[k], or_.at[place], dev)

    o_own = pltpu.make_async_copy(o_tx, out.at[:, mine], os_.at[16])
    for k in range(16):
        @pl.when(jnp.logical_not(jnp.logical_and(k == v, goal == w)))
        def _():
            result(k, mine, (k, goal)).start()

    @pl.when(goal == w)
    def _():
        o_own.start()

    for copy in sent:
        copy.wait_send()
    for k in range(16):
        @pl.when(jnp.logical_not(jnp.logical_and(2 * w + k // GROUPS == v, k % GROUPS == w)))
        def _():
            result(k, k, (v, w)).wait_recv()

        @pl.when(jnp.logical_not(jnp.logical_and(k == v, goal == w)))
        def _():
            result(k, mine, (k, goal)).wait_send()

    @pl.when(goal == w)
    def _():
        o_own.wait()


def on_device(hidden, norm_gain, head_weight, token_ids, seq_lengths):
    hbm = pl.BlockSpec(memory_space=pl.ANY)
    f32, bf16, i32 = jnp.float32, jnp.bfloat16, jnp.int32
    dma = pltpu.SemaphoreType.DMA
    rows = pltpu.VMEM((32, HALF, 128), f32)
    scores = pl.pallas_call(
        kernel,
        out_shape=jax.ShapeDtypeStruct((2, 16, 1, 128), f32),
        in_specs=[hbm, hbm, hbm, hbm, hbm],
        out_specs=hbm,
        scratch_shapes=[
            pltpu.VMEM((GROUPS, ROWS, 128), bf16),
            pltpu.VMEM((32, HALF, D), bf16),
            pltpu.VMEM((NCHUNK, CHUNK, D), bf16),
            pltpu.VMEM((GROUPS, 3, 128), f32),
            pltpu.VMEM((32, HALF, 128), i32),
            rows, rows, rows, rows,
            pltpu.VMEM((TILE, CHUNK), f32),
            pltpu.VMEM((TILE, CHUNK), f32),
            pltpu.VMEM((16, 4, 128), f32),
            pltpu.VMEM((32, 4, 128), f32),
            pltpu.VMEM((2, 1, 128), f32),
            pltpu.VMEM((1, SEQS), i32),
            pltpu.VMEM((1, 128), f32),
            pltpu.VMEM((2, GROUPS, 1, 128), i32),
            pltpu.VMEM((GROUPS, 3, 128), f32),
            dma((2, 8)), dma((2, 8)), dma((8,)), dma((8,)), dma((1,)),
            dma((40,)), dma((40,)), dma((72,)), dma((72,)), dma((8,)),
            dma((32,)), dma((32,)), dma((17,)), dma((16,)), dma((1,)),
        ],
        compiler_params=pltpu.CompilerParams(
            collective_id=0, has_side_effects=True, vmem_limit_bytes=56 * 2**20),
        name="score",
    )(hidden, head_weight.T, norm_gain.reshape(1, 128), token_ids.reshape(2, GROUPS, 1, 128),
      seq_lengths.reshape(1, SEQS))
    return scores[0].reshape(SEQ_LEN), scores[1].reshape(SEQ_LEN)


def solution(mesh):
    in_specs = (P("vocab", "width"), P("width"), P("width", "vocab"), P("width"), P())
    out_specs = (P("width"), P("width"))
    return jax.shard_map(
        on_device, mesh=mesh, in_specs=in_specs, out_specs=out_specs, check_vma=False
    )
```

time: 71.2 us -> 61.8 us (0.87)
  Pallas kernels: 66.4 us -> 59.6 us
  local copies, waits for them, and re-layouts: 3.96 us -> 1.32 us
    pallas_call x1, Pallas kernels: 66.4 us -> 59.6 us  [on_device(): pl.pallas_call(kernel, out_shape=jax.ShapeDtypeStruct((2, 16, 1, 128), f3...]
    unnamed x5 -> x0, local copies, waits for them, and re-layouts: 3.96 us -> none
    slice x0 -> x1, local copies, waits for them, and re-layouts: none -> 1.32 us  [on_device(): return (scores[0].reshape(SEQ_LEN), scores[1].reshape(SEQ_LEN))]
where the time goes in v2:
time: 61.8 us; the launch traced here: 61.6 us
  Pallas kernels  59.6 us (96%)
  local copies, waits for them, and re-layouts  1.32 us (2%)
  between operations  0.64 us (1%)
    pallas_call x1, Pallas kernels, on_device(): pl.pallas_call(kernel, out_shape=jax.ShapeDtypeStruct((2, 16, 1, 128), f3...  59.6 us
    slice x1, local copies, waits for them, and re-layouts, on_device(): return (scores[0].reshape(SEQ_LEN), scores[1].reshape(SEQ_LEN))  1.32 us

profile of v2, /device:TPU:1, one launch (start us, length us, event | category | flops | bytes accessed | tf_op | source)
XLA Modules:
  0.0 61.6 jit_solution(5752327621869209481)
XLA Ops:
  0.6 59.6 %score.1 = f32[2,16,1,128]{3,2,1,0:T(1,128)} custom-call(bf16[1024,128]{1,0:T(8,128)(2,1)} %hid.1, bf16[2008,128]{1,0:T(8,128)(2,1)} %bitcast.6, f32[1,128]{1,0:T(1,128)} %bitcast.10, s32[2,8,1,128]{3,2,1,0:T(1,128)} %bitcast.7, s32[1,8]{1,0:T(1,128)} %bitcast.11), custom_call_target="tpu_custom_call" | custom-call | tf_op jit(solution)/shard_map/score/pallas_call | solution.py:514
  60.2 1.3 %fusion = (f32[1,16,1,128]{3,2,1,0:T(1,128)}, f32[1,16,1,128]{3,2,1,0:T(1,128)}) fusion(f32[2,16,1,128]{3,2,1,0:T(1,128)} %score.1), kind=kLoop, calls=%fused_computation | loop fusion | bytes 32768 | tf_op jit(solution)/shard_map/slice | solution.py:544

commit v3 on v2

--- a/solution.py
+++ b/solution.py
@@ -226,11 +226,11 @@
                 X[h, "last", far, near].wait_recv()
 
     far_first = (3, 4, 2, 5, 1, 6, 0)
+    for copy in g_copies:
+        go(copy)
     for k in far_first:
         go(a_copies[0][k])
     w_own(0)
-    for copy in g_copies:
-        go(copy)
     for k in far_first:
         go(a_copies[1][k])
     w_own(1)
@@ -283,11 +283,13 @@
 
     w_forward(1)
     w_own(4)
+    w_forward(2)
     x_round1()
     x_near(1)
+    w_forward(3)
+    w_own(5)
     w_across(1)
-    w_forward(2)
-    w_own(5)
+    w_own(6)
     w_done(0)
 
     def pick(values, i):
@@ -335,17 +337,19 @@
             u[at_rows] = u_new
             t[at_rows] = t_new
 
-    def finish(q):
+    def finish(q, place=None):
+        place = q if place is None else place
+
         def rows_of(ref):
             return ref[pl.ds(q * 2, 2)].reshape(ROWS, 128).T
 
         mt = rows_of(m)
         peak = jnp.max(mt, axis=0, keepdims=True)
         scale = jnp.exp(mt - peak)
-        st_tx[q, 0:1, :] = peak
-        st_tx[q, 1:2, :] = jnp.sum(rows_of(s) * scale, axis=0, keepdims=True)
-        st_tx[q, 2:3, :] = jnp.sum(rows_of(u) * scale, axis=0, keepdims=True)
-        st_tx[q, 3:4, :] = jnp.sum(rows_of(t), axis=0, keepdims=True)
+        st_tx[place, 0:1, :] = peak
+        st_tx[place, 1:2, :] = jnp.sum(rows_of(s) * scale, axis=0, keepdims=True)
+        st_tx[place, 2:3, :] = jnp.sum(rows_of(u) * scale, axis=0, keepdims=True)
+        st_tx[place, 3:4, :] = jnp.sum(rows_of(t), axis=0, keepdims=True)
 
     S = {}
     for k, (h, dz, dx) in enumerate(UNITS):
@@ -363,40 +367,36 @@
         send_stats(tile)
 
     def acts_0():
-        w_forward(3)
-        w_own(6)
-        x_near(3)
-        x_pace()
-        w_across(2)
-        x_round2()
         w_forward(4)
         w_own(7)
+        w_across(2)
+        x_near(3)
+        w_across(3)
+        x_pace()
+        x_round2()
         x_round3_wait()
         x_round3()
 
     def acts_1():
-        w_across(3)
         w_forward(5)
+        w_forward(6)
+        w_across(4)
         w_done(1)
 
     def acts_2():
-        w_across(4)
-        x_round4(1)
-        w_forward(6)
-
-    def acts_3():
         w_across(5)
         w_forward(7)
+        x_round4(1)
+
+    def acts_3():
+        w_across(6)
         w_done(2)
 
     def acts_4():
+        w_across(7)
         x_round4(3)
 
-    def acts_5():
-        w_across(6)
-
     def acts_6():
-        w_across(7)
         x_round5()
 
     def acts_7():
@@ -404,43 +404,55 @@
 
     def acts_8():
         x_last(0)
-        finish_tile(4)
 
     def acts_9():
-        finish_tile(3)
-        finish_tile(2)
+        send_stats(4)
 
     def acts_10():
+        send_stats(3)
         x_last(1)
 
     def acts_11():
-        finish_tile(5)
+        send_stats(2)
 
     def acts_12():
+        send_stats(5)
         x_last(3)
         x_last(2)
 
-    def acts_13():
-        finish_tile(6)
-
-    def acts_15():
-        finish_tile(7)
-
-    ACTS = {0: acts_0, 1: acts_1, 2: acts_2, 3: acts_3, 4: acts_4, 5: acts_5, 6: acts_6, 7: acts_7, 8: acts_8,
-            9: acts_9, 10: acts_10, 11: acts_11, 12: acts_12, 13: acts_13, 15: acts_15}
+    def acts_14():
+        send_stats(6)
+
+    EARLY = {0: acts_0, 1: acts_1, 2: acts_2, 3: acts_3, 4: acts_4, 6: acts_6, 7: acts_7}
+    LATE = {8: acts_8, 9: acts_9, 10: acts_10, 11: acts_11, 12: acts_12, 14: acts_14}
+    READY = [4, 3, 2, 5, 8, 6, 8, 7]
     total = len(STEPS)
     dot(0, lb0)
 
-    @pl.loop(0, total // 2)
-    def _(h):
+    def block(h):
         i = h * 2
-        for k in ACTS:
-            pl.when(h == k)(ACTS[k])
         dot(i + 1, lb1)
         stats(i, lb0)
         dot(jnp.minimum(i + 2, total - 1), lb0)
         stats(i + 1, lb1)
 
+    @pl.loop(0, 8)
+    def _(h):
+        for k in EARLY:
+            pl.when(h == k)(EARLY[k])
+        block(h)
+
+    @pl.loop(8, total // 2)
+    def _(h):
+        for k in LATE:
+            pl.when(h == k)(LATE[k])
+        place = pick(READY, h - 8) * 2
+        source = jnp.minimum(place, 14)
+        finish(source, place)
+        finish(source + 1, place + 1)
+        block(h)
+
+    send_stats(7)
     for tile in (1, 0):
         finish_tile(tile)
     for copy in S.values():
@@ -525,7 +537,7 @@
             rows, rows, rows, rows,
             pltpu.VMEM((TILE, CHUNK), f32),
             pltpu.VMEM((TILE, CHUNK), f32),
-            pltpu.VMEM((16, 4, 128), f32),
+            pltpu.VMEM((18, 4, 128), f32),
             pltpu.VMEM((32, 4, 128), f32),
             pltpu.VMEM((2, 1, 128), f32),
             pltpu.VMEM((1, SEQS), i32),

time: 61.8 us -> 59.8 us (0.968)
  Pallas kernels: 59.6 us -> 57.7 us
    pallas_call x1, Pallas kernels: 59.6 us -> 57.7 us  [on_device(): pl.pallas_call(kernel, out_shape=jax.ShapeDtypeStruct((2, 16, 1, 128), f3...]
where the time goes in v3:
time: 59.8 us; the launch traced here: 59.6 us
  Pallas kernels  57.7 us (96%)
  local copies, waits for them, and re-layouts  1.32 us (2%)
  between operations  0.64 us (1%)
    pallas_call x1, Pallas kernels, on_device(): pl.pallas_call(kernel, out_shape=jax.ShapeDtypeStruct((2, 16, 1, 128), f3...  57.7 us
    slice x1, local copies, waits for them, and re-layouts, on_device(): return (scores[0].reshape(SEQ_LEN), scores[1].reshape(SEQ_LEN))  1.32 us

profile of v3, /device:TPU:1, one launch (start us, length us, event | category | flops | bytes accessed | tf_op | source)
XLA Modules:
  0.0 59.6 jit_solution(6652970758534608293)
XLA Ops:
  0.6 57.7 %score.1 = f32[2,16,1,128]{3,2,1,0:T(1,128)} custom-call(bf16[1024,128]{1,0:T(8,128)(2,1)} %hid.1, bf16[2008,128]{1,0:T(8,128)(2,1)} %bitcast.6, f32[1,128]{1,0:T(1,128)} %bitcast.10, s32[2,8,1,128]{3,2,1,0:T(1,128)} %bitcast.7, s32[1,8]{1,0:T(1,128)} %bitcast.11), custom_call_target="tpu_custom_call" | custom-call | tf_op jit(solution)/shard_map/score/pallas_call | solution.py:526
  58.3 1.3 %fusion = (f32[1,16,1,128]{3,2,1,0:T(1,128)}, f32[1,16,1,128]{3,2,1,0:T(1,128)}) fusion(f32[2,16,1,128]{3,2,1,0:T(1,128)} %score.1), kind=kLoop, calls=%fused_computation | loop fusion | bytes 32768 | tf_op jit(solution)/shard_map/slice | solution.py:556

commit v4 on v3

--- a/solution.py
+++ b/solution.py
@@ -29,8 +29,8 @@
 NTILE = 8
 STEPS = [(0, 0), (1, 0), (2, 0), (0, 1), (1, 1), (2, 1), (3, 0), (3, 1),
          (0, 2), (1, 2), (2, 2), (3, 2), (4, 0), (4, 1), (4, 2), (4, 3),
-         (3, 3), (2, 3), (5, 0), (5, 1), (5, 2), (5, 3), (6, 0), (6, 1),
-         (6, 2), (6, 3), (7, 0), (7, 1), (7, 2), (7, 3), (1, 3), (0, 3)]
+         (5, 0), (5, 1), (5, 2), (5, 3), (6, 0), (6, 1), (6, 2), (6, 3),
+         (7, 0), (7, 1), (7, 2), (7, 3), (3, 3), (2, 3), (1, 3), (0, 3)]
 PART = 256
 NPART = 8
 
@@ -384,8 +384,8 @@
         w_done(1)
 
     def acts_2():
+        w_forward(7)
         w_across(5)
-        w_forward(7)
         x_round4(1)
 
     def acts_3():
@@ -393,39 +393,31 @@
         w_done(2)
 
     def acts_4():
+        x_round4(3)
+
+    def acts_5():
         w_across(7)
-        x_round4(3)
-
-    def acts_6():
+
+    def acts_7():
         x_round5()
-
-    def acts_7():
         w_done(3)
-
-    def acts_8():
         x_last(0)
 
     def acts_9():
         send_stats(4)
-
-    def acts_10():
-        send_stats(3)
         x_last(1)
 
     def acts_11():
-        send_stats(2)
-
-    def acts_12():
         send_stats(5)
         x_last(3)
         x_last(2)
 
-    def acts_14():
+    def acts_13():
         send_stats(6)
 
-    EARLY = {0: acts_0, 1: acts_1, 2: acts_2, 3: acts_3, 4: acts_4, 6: acts_6, 7: acts_7}
-    LATE = {8: acts_8, 9: acts_9, 10: acts_10, 11: acts_11, 12: acts_12, 14: acts_14}
-    READY = [4, 3, 2, 5, 8, 6, 8, 7]
+    EARLY = {0: acts_0, 1: acts_1, 2: acts_2, 3: acts_3, 4: acts_4, 5: acts_5, 7: acts_7}
+    LATE = {9: acts_9, 11: acts_11, 13: acts_13}
+    READY = [4, 8, 5, 8, 6, 8, 7]
     total = len(STEPS)
     dot(0, lb0)
 
@@ -442,7 +434,7 @@
             pl.when(h == k)(EARLY[k])
         block(h)
 
-    @pl.loop(8, total // 2)
+    @pl.loop(8, total // 2 - 1)
     def _(h):
         for k in LATE:
             pl.when(h == k)(LATE[k])
@@ -453,6 +445,11 @@
         block(h)
 
     send_stats(7)
+    for q in (6, 7, 4, 5):
+        finish(q)
+    block(total // 2 - 1)
+    send_stats(3)
+    send_stats(2)
     for tile in (1, 0):
         finish_tile(tile)
     for copy in S.values():

time: 59.8 us -> 58.4 us (0.977)
  Pallas kernels: 57.7 us -> 56.3 us
    pallas_call x1, Pallas kernels: 57.7 us -> 56.3 us  [on_device(): pl.pallas_call(kernel, out_shape=jax.ShapeDtypeStruct((2, 16, 1, 128), f3...]
where the time goes in v4:
time: 58.4 us; the launch traced here: 58.2 us
  Pallas kernels  56.3 us (96%)
  local copies, waits for them, and re-layouts  1.32 us (2%)
  between operations  0.64 us (1%)
    pallas_call x1, Pallas kernels, on_device(): pl.pallas_call(kernel, out_shape=jax.ShapeDtypeStruct((2, 16, 1, 128), f3...  56.3 us
    slice x1, local copies, waits for them, and re-layouts, on_device(): return (scores[0].reshape(SEQ_LEN), scores[1].reshape(SEQ_LEN))  1.32 us

profile of v4, /device:TPU:1, one launch (start us, length us, event | category | flops | bytes accessed | tf_op | source)
XLA Modules:
  0.0 58.2 jit_solution(10755185991421798436)
XLA Ops:
  0.6 56.3 %score.1 = f32[2,16,1,128]{3,2,1,0:T(1,128)} custom-call(bf16[1024,128]{1,0:T(8,128)(2,1)} %hid.1, bf16[2008,128]{1,0:T(8,128)(2,1)} %bitcast.6, f32[1,128]{1,0:T(1,128)} %bitcast.10, s32[2,8,1,128]{3,2,1,0:T(1,128)} %bitcast.7, s32[1,8]{1,0:T(1,128)} %bitcast.11), custom_call_target="tpu_custom_call" | custom-call | tf_op jit(solution)/shard_map/score/pallas_call | solution.py:523
  56.9 1.3 %fusion = (f32[1,16,1,128]{3,2,1,0:T(1,128)}, f32[1,16,1,128]{3,2,1,0:T(1,128)}) fusion(f32[2,16,1,128]{3,2,1,0:T(1,128)} %score.1), kind=kLoop, calls=%fused_computation | loop fusion | bytes 32768 | tf_op jit(solution)/shard_map/slice | solution.py:553
